TPU v7x, 1024 devices: a whole 8x8x8 slice. The times are simulated.
1024 devices in a mesh: gx: 16 (over z, core), gy: 64 (over y, x).
Axes of the slice: x: 8, y: 8, z: 8, core: 2. Of those that a mesh axis runs over, the one named last changes fastest.
Arguments:
- particles: float32 [12288, 6, 128], P(('gx', 'gy')), may hold values from -6 to 6
- occupancy: int32 [12288], P(('gx', 'gy')), may hold values from 32 to 128, as said below
- neighbours: int32 [12288, 16], P(('gx', 'gy')), may hold values from 0 to 12287, as said below
- curve_cuts: int32 [2, 1024], replicated, may hold values from 0 to 12282, as said below
Outputs:
- after_first: float32 [24576, 6, 128], P(('gx', 'gy'))
- after_second: float32 [24576, 6, 128], P(('gx', 'gy'))
Inputs may be any that keep to these rules, and one draw needn't show every extreme that they name: `occupancy`: each tile holds at least 32 live particles, and some tile in every draw holds 128. `neighbours`: tile t lists 16 different tiles among the curve positions t + 1 to t + 24, counted modulo 12288. `curve_cuts`: entry d of each row is d * 12 + e with e between -6 and 6, and e is 0 for device 0; so each device owns 0 to 24 tiles, and in every step some device owns exactly 24.
All inputs are finite; a program needn't handle non-finite values.
Results may differ from a plain program's by a relative error of at most 0.0001.
Values sent between devices are 32-bit elements; how exact they have to be, the bound alone decides.
A program may use at most 32 MiB of HBM per device.

v0:
```python
import jax
import jax.numpy as jnp
from jax import lax
from jax.sharding import PartitionSpec as P

TILE_P = 128
STEPS = 2


soften = 0.05
time_step = 0.5
group_tiles = 2


def shifted(value, axis, steps):
    count = lax.axis_size(axis)
    first, last = (max(0, -steps), min(count, count - steps))
    return lax.ppermute(value, axis, [(source, source + steps) for source in range(first, last)])


def shifted_2(value, axis, steps):
    count = lax.axis_size(axis)
    pairs = [(source, (source + steps) % count) for source in range(count)]
    return lax.ppermute(value, axis, pairs)


def pair_terms(targets, sources):
    target_pos = targets[:, None, :3, :, None]
    source_pos = sources[:, :, :3, None, :]
    separation = source_pos - target_pos
    distance_sq = jnp.sum(separation * separation, axis=2) + soften
    kernel = distance_sq ** (-1.5)
    action = jnp.sum(
        kernel[:, :, None] * sources[:, :, 3][:, :, None, None, :] * separation, axis=(1, 4)
    )
    reaction = -jnp.sum(
        kernel[:, :, None] * targets[:, 3][:, None, None, :, None] * separation, axis=3
    )
    return (action, reaction)


def pair_scan(own_pos, tile_pool, source_index):
    tile_count = own_pos.shape[0]
    slot_count = own_pos.shape[2]
    group_count = tile_count // group_tiles

    def block_pass(react_pool, inputs):
        targets, source_ids = inputs
        sources = jnp.concatenate(
            [targets[:, None], jnp.take(tile_pool, source_ids, axis=0)], axis=1
        )
        action, reaction = pair_terms(targets, sources)
        react_pool = react_pool.at[source_ids.reshape(-1)].add(
            reaction[:, 1:].reshape(-1, 3, slot_count)
        )
        return (react_pool, action)

    start_pool = jnp.zeros((tile_pool.shape[0], 3, slot_count), jnp.float32)
    react_pool, actions = lax.scan(
        block_pass,
        start_pool,
        (
            own_pos.reshape(group_count, group_tiles, 4, slot_count),
            source_index.reshape(group_count, group_tiles, -1),
        ),
    )
    return (actions.reshape(tile_count, 3, slot_count), react_pool)


def relocate(tile_rows, offsets, old_starts, new_starts, device):
    capacity = tile_rows.shape[0]
    prev_old = old_starts[jnp.maximum(device - 1, 0)]
    own_old = old_starts[device]
    next_old = old_starts[device + 1]
    own_new = new_starts[device]
    next_new = new_starts[device + 1]
    lower_rows, lower_offsets = shifted((tile_rows, offsets), ("gx", "gy"), 1)
    upper_rows, upper_offsets = shifted((tile_rows, offsets), ("gx", "gy"), -1)
    lower_count = lower_rows.shape[0]
    upper_count = upper_rows.shape[0]
    pool_rows = jnp.concatenate([lower_rows, tile_rows, upper_rows], axis=0)
    pool_offsets = jnp.concatenate([lower_offsets, offsets, upper_offsets], axis=0)
    wanted = own_new + jnp.arange(capacity, dtype=jnp.int32)
    filled = (wanted < next_new).astype(jnp.float32)
    from_lower = wanted < own_old
    from_own = wanted < next_old
    source_index = jnp.where(
        from_lower,
        wanted - prev_old,
        jnp.where(
            from_own, lower_count + wanted - own_old, lower_count + capacity + wanted - next_old
        ),
    )
    source_index = jnp.clip(source_index, 0, lower_count + capacity + upper_count - 1)
    moved_rows = jnp.take(pool_rows, source_index, axis=0) * filled[:, None, None]
    moved_offsets = jnp.take(pool_offsets, source_index, axis=0) * filled[:, None]
    return (moved_rows, moved_offsets)


def tile_forces(tile_rows, offsets, starts, device, mesh_size, total_tiles):
    capacity = tile_rows.shape[0]
    own_pos = jnp.concatenate([tile_rows[:, :3], tile_rows[:, 6:7]], axis=1)
    windows = [own_pos]
    for distance in range(1, 4):
        windows.append(shifted_2(own_pos, ("gx", "gy"), -distance))
    tile_pool = jnp.concatenate(windows, axis=0)
    first_tiles = []
    for distance in range(4):
        device_index = device + distance
        first_tiles.append(
            starts[device_index % mesh_size] + device_index // mesh_size * total_tiles
        )
    first_table = jnp.stack(first_tiles)
    wanted = (
        first_tiles[0] + jnp.arange(capacity, dtype=jnp.int32)[:, None] + offsets.astype(jnp.int32)
    )
    segment = (
        (wanted >= first_tiles[1]).astype(jnp.int32)
        + (wanted >= first_tiles[2]).astype(jnp.int32)
        + (wanted >= first_tiles[3]).astype(jnp.int32)
    )
    source_index = jnp.clip(
        segment * capacity + wanted - jnp.take(first_table, segment), 0, 4 * capacity - 1
    )
    actions, react_pool = pair_scan(own_pos, tile_pool, source_index)
    acceleration = actions + react_pool[:capacity]
    for distance in range(1, 4):
        returned = shifted_2(
            react_pool[distance * capacity : (distance + 1) * capacity], ("gx", "gy"), distance
        )
        acceleration = acceleration + returned
    return acceleration


def body(particles, occupancy, neighbours, curve_cuts):
    device = lax.axis_index(("gx", "gy"))
    mesh_size = lax.axis_size(("gx", "gy"))
    tiles_home = particles.shape[0]
    slot_count = particles.shape[2]
    total_tiles = tiles_home * mesh_size
    capacity = 2 * tiles_home
    slot_ids = jnp.arange(slot_count, dtype=jnp.int32)
    weight = (slot_ids[None, :] < occupancy[:, None]).astype(jnp.float32)
    home_tiles = device * tiles_home + jnp.arange(tiles_home, dtype=jnp.int32)
    home_offsets = (neighbours - home_tiles[:, None]) % total_tiles
    tail_entry = jnp.array([total_tiles], jnp.int32)
    snapshots = []
    offsets = home_offsets.astype(jnp.float32)
    padding = capacity - tiles_home
    tile_rows = jnp.pad(
        jnp.concatenate([particles, weight[:, None]], axis=1), ((0, padding), (0, 0), (0, 0))
    )
    offsets = jnp.pad(offsets, ((0, padding), (0, 0)))
    old_starts = jnp.arange(mesh_size + 1, dtype=jnp.int32) * tiles_home
    for step_index in range(STEPS):
        new_starts = jnp.concatenate([curve_cuts[step_index], tail_entry])
        tile_rows, offsets = relocate(tile_rows, offsets, old_starts, new_starts, device)
        acceleration = tile_forces(tile_rows, offsets, new_starts, device, mesh_size, total_tiles)
        live_weight = tile_rows[:, 6:7]
        velocity = live_weight * (tile_rows[:, 3:6] + time_step * acceleration / TILE_P)
        position = live_weight * (tile_rows[:, :3] + time_step * velocity)
        tile_rows = jnp.concatenate([position, velocity, live_weight], axis=1)
        snapshots.append(jnp.concatenate([position, velocity], axis=1))
        old_starts = new_starts
    return (snapshots[0], snapshots[1])


def solution(mesh):
    in_specs = (P(("gx", "gy"), None, None), P(("gx", "gy")), P(("gx", "gy"), None), P())
    out_specs = (P(("gx", "gy"), None, None), P(("gx", "gy"), None, None))
    return jax.shard_map(body, mesh=mesh, in_specs=in_specs, out_specs=out_specs, check_vma=False)
```

profile of v0, /device:TPU:514, one launch (start us, length us, event | category | flops | bytes accessed | tf_op | source)
XLA Modules:
  0.0 293.8 jit_solution(1290358898106729987)
XLA Ops:
  1.5 2.4 collective-permute-start.3
  3.9 3.4 %collective-permute-start.2 = (f32[24,16]{0,1:T(8,128)S(1)}, f32[24,16]{0,1:T(8,128)S(1)}, u32[]{:S(2)}, u32[]{:S(2)}) collective-permute-start(f32[24,16]{0,1:T(8,128)S(1)} %pad.9), channel_id=1, source_target_pairs={{0,1},{1,2},{2,3},{3,4},{4,5},{5,6},{6,7},{7,8},{8,9},{9,10},{10,1... | collective-permute-start | bytes 4616 | tf_op jit(solution)/shard_map/ppermute | solution.py:18
  8.9 4.6 %collective-permute-start.1 = (f32[24,7,128]{2,1,0:T(8,128)S(1)}, f32[24,7,128]{2,1,0:T(8,128)S(1)}, u32[]{:S(2)}, u32[]{:S(2)}) collective-permute-start(f32[24,7,128]{2,1,0:T(8,128)S(1)} %select_maximum_fusion), channel_id=1, source_target_pairs={{1,0},{2,1},{3,2},{4,3},{5,4},{6,5},{7,6},{8,7},{9,8},{10,9},{11,1... | collective-permute-start | bytes 258056 | tf_op jit(solution)/shard_map/ppermute | solution.py:18
  13.5 1.9 collective-permute-start
  31.9 9.7 %collective-permute-start.6 = (f32[24,4,128]{2,1,0:T(4,128)S(1)}, f32[24,4,128]{2,1,0:T(4,128)S(1)}, u32[]{:S(2)}, u32[]{:S(2)}) collective-permute-start(f32[24,4,128]{2,1,0:T(4,128)S(1)} %pad_maximum_fusion.9), channel_id=1, source_target_pairs={{0,1021},{1,1022},{2,1023},{3,0},{4,1},{5,2},{6,3},{7,4},{8,5},{9,... | collective-permute-start | bytes 147464 | tf_op jit(solution)/shard_map/ppermute | solution.py:24
  41.6 7.9 %collective-permute-start.5 = (f32[24,4,128]{2,1,0:T(4,128)S(1)}, f32[24,4,128]{2,1,0:T(4,128)S(1)}, u32[]{:S(2)}, u32[]{:S(2)}) collective-permute-start(f32[24,4,128]{2,1,0:T(4,128)S(1)} %pad_maximum_fusion.9), channel_id=1, source_target_pairs={{0,1022},{1,1023},{2,0},{3,1},{4,2},{5,3},{6,4},{7,5},{8,6},{9,7},... | collective-permute-start | bytes 147464 | tf_op jit(solution)/shard_map/ppermute | solution.py:24
  49.5 1.9 collective-permute-start.4
  51.5 3.9 %collective-permute-done.4 = f32[24,4,128]{2,1,0:T(4,128)S(1)} collective-permute-done((f32[24,4,128]{2,1,0:T(4,128)S(1)}, f32[24,4,128]{2,1,0:T(4,128)S(1)}, u32[]{:S(2)}, u32[]{:S(2)}) %collective-permute-start.4) | collective-permute-done | bytes 49184 | tf_op jit(solution)/shard_map/ppermute | solution.py:24
  55.6 78.7 %while.24 = (s32[]{:T(128)}, f32[96,3,128]{2,1,0:T(4,128)S(1)}, f32[12,2,3,128]{3,2,1,0:T(4,128)S(1)}, s32[12,2,16]{2,1,0:T(2,128)S(1)}, f32[12,2,4,128]{3,2,1,0...) while((s32[]{:T(128)}, f32[96,3,128]{2,1,0:T(4,128)S(1)}, f32[12,2,3,128]{3,2,1,0:T(4,128)S(1)}, ...), condition=%wide.region_5.10_spmd, body=%wide.region_0.9_spmd.sunk | while | flops 14529410 | bytes 14446433 | solution.py:59
  58.5 1.8 fusion.58
  65.0 1.8 fusion.58
  71.5 1.8 fusion.58
  73.4 1.7 scatter_fusion
  78.1 1.8 fusion.58
  80.0 1.7 scatter_fusion
  84.7 1.8 fusion.58
  86.5 1.7 scatter_fusion
  91.2 1.8 fusion.58
  93.1 1.7 scatter_fusion
  97.8 1.8 fusion.58
  99.7 1.7 scatter_fusion
  104.4 1.8 fusion.58
  106.3 1.7 scatter_fusion
  111.0 1.8 fusion.58
  112.8 1.7 scatter_fusion
  117.5 1.8 fusion.58
  119.4 1.7 scatter_fusion
  124.1 1.8 fusion.58
  126.0 1.7 scatter_fusion
  130.7 1.8 fusion.58
  132.6 1.7 scatter_fusion
  134.4 3.5 %collective-permute-start.7 = (f32[24,3,128]{2,1,0:T(4,128)S(1)}, f32[24,3,128]{2,1,0:T(4,128)S(1)}, u32[]{:S(2)}, u32[]{:S(2)}) collective-permute-start(f32[24,3,128]{2,1,0:T(4,128)S(1)} %get-tuple-element.163), channel_id=1, source_target_pairs={{0,1},{1,2},{2,3},{3,4},{4,5},{5,6},{6,7},{7,8},{8,9},{9,10},{10,1... | collective-permute-start | bytes 110600 | tf_op jit(solution)/shard_map/ppermute | solution.py:24
  137.9 5.1 %collective-permute-start.9 = (f32[24,3,128]{2,1,0:T(4,128)S(1)}, f32[24,3,128]{2,1,0:T(4,128)S(1)}, u32[]{:S(2)}, u32[]{:S(2)}) collective-permute-start(f32[24,3,128]{2,1,0:T(4,128)S(1)} %get-tuple-element.164), channel_id=1, source_target_pairs={{0,3},{1,4},{2,5},{3,6},{4,7},{5,8},{6,9},{7,10},{8,11},{9,12},{10... | collective-permute-start | bytes 110600 | tf_op jit(solution)/shard_map/ppermute | solution.py:24
  143.0 2.5 collective-permute-start.8
  149.2 3.4 %collective-permute-start.13 = (f32[24,16]{1,0:T(8,128)S(1)}, f32[24,16]{1,0:T(8,128)S(1)}, u32[]{:S(2)}, u32[]{:S(2)}) collective-permute-start(f32[24,16]{1,0:T(8,128)S(1)} %get-tuple-element.149), channel_id=1, source_target_pairs={{1,0},{2,1},{3,2},{4,3},{5,4},{6,5},{7,6},{8,7},{9,8},{10,9},{11,1... | collective-permute-start | bytes 4616 | tf_op jit(solution)/shard_map/ppermute | solution.py:18
  152.6 2.5 collective-permute-start.12
  155.2 8.0 %collective-permute-start.11 = (f32[24,7,128]{2,1,0:T(8,128)S(1)}, f32[24,7,128]{2,1,0:T(8,128)S(1)}, u32[]{:S(2)}, u32[]{:S(2)}) collective-permute-start(f32[24,7,128]{2,1,0:T(8,128)S(1)} %pad_maximum_fusion.7), channel_id=1, source_target_pairs={{1,0},{2,1},{3,2},{4,3},{5,4},{6,5},{7,6},{8,7},{9,8},{10,9},{11,1... | collective-permute-start | bytes 258056 | tf_op jit(solution)/shard_map/ppermute | solution.py:18
  163.2 1.9 collective-permute-start.10
  165.7 9.1 %collective-permute-done.10 = f32[24,7,128]{2,1,0:T(8,128)S(1)} collective-permute-done((f32[24,7,128]{2,1,0:T(8,128)S(1)}, f32[24,7,128]{2,1,0:T(8,128)S(1)}, u32[]{:S(2)}, u32[]{:S(2)}) %collective-permute-start.10) | collective-permute-done | bytes 86048 | tf_op jit(solution)/shard_map/ppermute | solution.py:18
  175.7 2.5 collective-permute-start.16
  178.2 7.0 %collective-permute-start.15 = (f32[24,4,128]{2,1,0:T(4,128)S(1)}, f32[24,4,128]{2,1,0:T(4,128)S(1)}, u32[]{:S(2)}, u32[]{:S(2)}) collective-permute-start(f32[24,4,128]{2,1,0:T(4,128)S(1)} %pad_maximum_fusion.10), channel_id=1, source_target_pairs={{0,1022},{1,1023},{2,0},{3,1},{4,2},{5,3},{6,4},{7,5},{8,6},{9,7},... | collective-permute-start | bytes 147464 | tf_op jit(solution)/shard_map/ppermute | solution.py:24
  185.2 3.1 %collective-permute-start.14 = (f32[24,4,128]{2,1,0:T(4,128)S(1)}, f32[24,4,128]{2,1,0:T(4,128)S(1)}, u32[]{:S(2)}, u32[]{:S(2)}) collective-permute-start(f32[24,4,128]{2,1,0:T(4,128)S(1)} %pad_maximum_fusion.10), channel_id=1, source_target_pairs={{0,1023},{1,0},{2,1},{3,2},{4,3},{5,4},{6,5},{7,6},{8,7},{9,8},{10... | collective-permute-start | bytes 147464 | tf_op jit(solution)/shard_map/ppermute | solution.py:24
  188.4 2.4 collective-permute-done.15
  191.9 78.1 %while.25 = (s32[]{:T(128)}, f32[96,3,128]{2,1,0:T(4,128)S(1)}, f32[12,2,3,128]{3,2,1,0:T(4,128)S(1)}, s32[12,2,16]{2,1,0:T(2,128)S(1)}, f32[12,2,4,128]{3,2,1,0...) while((s32[]{:T(128)}, f32[96,3,128]{2,1,0:T(4,128)S(1)}, f32[12,2,3,128]{3,2,1,0:T(4,128)S(1)}, ...), condition=%wide.region_11.16_spmd, body=%wide.region_6.15_spmd.sunk | while | flops 14529410 | bytes 14446433 | solution.py:59
  194.9 1.8 fusion.64
  201.4 1.8 fusion.64
  207.9 1.8 fusion.64
  214.4 1.8 fusion.64
  220.8 1.8 fusion.64
  227.3 1.8 fusion.64
  233.8 1.8 fusion.64
  240.3 1.8 fusion.64
  246.8 1.8 fusion.64
  253.3 1.8 fusion.64
  255.2 1.7 scatter_fusion.1
  259.9 1.8 fusion.64
  261.7 1.7 scatter_fusion.1
  266.4 1.8 fusion.64
  268.3 1.7 scatter_fusion.1
  270.1 4.3 %collective-permute-start.17 = (f32[24,3,128]{2,1,0:T(4,128)S(1)}, f32[24,3,128]{2,1,0:T(4,128)S(1)}, u32[]{:S(2)}, u32[]{:S(2)}) collective-permute-start(f32[24,3,128]{2,1,0:T(4,128)S(1)} %get-tuple-element.160), channel_id=1, source_target_pairs={{0,1},{1,2},{2,3},{3,4},{4,5},{5,6},{6,7},{7,8},{8,9},{9,10},{10,1... | collective-permute-start | bytes 110600 | tf_op jit(solution)/shard_map/ppermute | solution.py:24
  274.5 6.4 %collective-permute-start.19 = (f32[24,3,128]{2,1,0:T(4,128)S(1)}, f32[24,3,128]{2,1,0:T(4,128)S(1)}, u32[]{:S(2)}, u32[]{:S(2)}) collective-permute-start(f32[24,3,128]{2,1,0:T(4,128)S(1)} %get-tuple-element.161), channel_id=1, source_target_pairs={{0,3},{1,4},{2,5},{3,6},{4,7},{5,8},{6,9},{7,10},{8,11},{9,12},{10... | collective-permute-start | bytes 110600 | tf_op jit(solution)/shard_map/ppermute | solution.py:24
  280.8 1.9 collective-permute-start.18
  283.4 4.2 %collective-permute-done.19 = f32[24,3,128]{2,1,0:T(4,128)S(1)} collective-permute-done((f32[24,3,128]{2,1,0:T(4,128)S(1)}, f32[24,3,128]{2,1,0:T(4,128)S(1)}, u32[]{:S(2)}, u32[]{:S(2)}) %collective-permute-start.19) | collective-permute-done | bytes 36896 | tf_op jit(solution)/shard_map/ppermute | solution.py:24
  287.6 5.5 %collective-permute-done.18 = f32[24,3,128]{2,1,0:T(4,128)S(1)} collective-permute-done((f32[24,3,128]{2,1,0:T(4,128)S(1)}, f32[24,3,128]{2,1,0:T(4,128)S(1)}, u32[]{:S(2)}, u32[]{:S(2)}) %collective-permute-start.18) | collective-permute-done | bytes 36896 | tf_op jit(solution)/shard_map/ppermute | solution.py:24
  (557 shorter events, 98.1 us)
Async XLA Ops:
  1.5 28.8 %collective-permute-start.3 = (f32[24,16]{0,1:T(8,128)S(1)}, f32[24,16]{0,1:T(8,128)S(1)}, u32[]{:S(2)}, u32[]{:S(2)}) collective-permute-start(f32[24,16]{0,1:T(8,128)S(1)} %pad.9), channel_id=1, source_target_pairs={{1,0},{2,1},{3,2},{4,3},{5,4},{6,5},{7,6},{8,7},{9,8},{10,9},{11,1... | collective-permute-start | bytes 4616 | tf_op jit(solution)/shard_map/ppermute | solution.py:18
  3.9 26.4 %collective-permute-start.2 = (f32[24,16]{0,1:T(8,128)S(1)}, f32[24,16]{0,1:T(8,128)S(1)}, u32[]{:S(2)}, u32[]{:S(2)}) collective-permute-start(f32[24,16]{0,1:T(8,128)S(1)} %pad.9), channel_id=1, source_target_pairs={{0,1},{1,2},{2,3},{3,4},{4,5},{5,6},{6,7},{7,8},{8,9},{9,10},{10,1... | collective-permute-start | bytes 4616 | tf_op jit(solution)/shard_map/ppermute | solution.py:18
  8.9 22.2 %collective-permute-start.1 = (f32[24,7,128]{2,1,0:T(8,128)S(1)}, f32[24,7,128]{2,1,0:T(8,128)S(1)}, u32[]{:S(2)}, u32[]{:S(2)}) collective-permute-start(f32[24,7,128]{2,1,0:T(8,128)S(1)} %select_maximum_fusion), channel_id=1, source_target_pairs={{1,0},{2,1},{3,2},{4,3},{5,4},{6,5},{7,6},{8,7},{9,8},{10,9},{11,1... | collective-permute-start | bytes 258056 | tf_op jit(solution)/shard_map/ppermute | solution.py:18
  13.5 17.5 %collective-permute-start = (f32[24,7,128]{2,1,0:T(8,128)S(1)}, f32[24,7,128]{2,1,0:T(8,128)S(1)}, u32[]{:S(2)}, u32[]{:S(2)}) collective-permute-start(f32[24,7,128]{2,1,0:T(8,128)S(1)} %select_maximum_fusion), channel_id=1, source_target_pairs={{0,1},{1,2},{2,3},{3,4},{4,5},{5,6},{6,7},{7,8},{8,9},{9,10},{10,1... | collective-permute-start | bytes 258056 | tf_op jit(solution)/shard_map/ppermute | solution.py:18
  31.9 19.6 %collective-permute-start.6 = (f32[24,4,128]{2,1,0:T(4,128)S(1)}, f32[24,4,128]{2,1,0:T(4,128)S(1)}, u32[]{:S(2)}, u32[]{:S(2)}) collective-permute-start(f32[24,4,128]{2,1,0:T(4,128)S(1)} %pad_maximum_fusion.9), channel_id=1, source_target_pairs={{0,1021},{1,1022},{2,1023},{3,0},{4,1},{5,2},{6,3},{7,4},{8,5},{9,... | collective-permute-start | bytes 147464 | tf_op jit(solution)/shard_map/ppermute | solution.py:24
  41.6 9.9 %collective-permute-start.5 = (f32[24,4,128]{2,1,0:T(4,128)S(1)}, f32[24,4,128]{2,1,0:T(4,128)S(1)}, u32[]{:S(2)}, u32[]{:S(2)}) collective-permute-start(f32[24,4,128]{2,1,0:T(4,128)S(1)} %pad_maximum_fusion.9), channel_id=1, source_target_pairs={{0,1022},{1,1023},{2,0},{3,1},{4,2},{5,3},{6,4},{7,5},{8,6},{9,7},... | collective-permute-start | bytes 147464 | tf_op jit(solution)/shard_map/ppermute | solution.py:24
  49.5 6.0 %collective-permute-start.4 = (f32[24,4,128]{2,1,0:T(4,128)S(1)}, f32[24,4,128]{2,1,0:T(4,128)S(1)}, u32[]{:S(2)}, u32[]{:S(2)}) collective-permute-start(f32[24,4,128]{2,1,0:T(4,128)S(1)} %pad_maximum_fusion.9), channel_id=1, source_target_pairs={{0,1023},{1,0},{2,1},{3,2},{4,3},{5,4},{6,5},{7,6},{8,7},{9,8},{10... | collective-permute-start | bytes 147464 | tf_op jit(solution)/shard_map/ppermute | solution.py:24
  134.4 20.7 %collective-permute-start.7 = (f32[24,3,128]{2,1,0:T(4,128)S(1)}, f32[24,3,128]{2,1,0:T(4,128)S(1)}, u32[]{:S(2)}, u32[]{:S(2)}) collective-permute-start(f32[24,3,128]{2,1,0:T(4,128)S(1)} %get-tuple-element.163), channel_id=1, source_target_pairs={{0,1},{1,2},{2,3},{3,4},{4,5},{5,6},{6,7},{7,8},{8,9},{9,10},{10,1... | collective-permute-start | bytes 110600 | tf_op jit(solution)/shard_map/ppermute | solution.py:24
  137.9 17.2 %collective-permute-start.9 = (f32[24,3,128]{2,1,0:T(4,128)S(1)}, f32[24,3,128]{2,1,0:T(4,128)S(1)}, u32[]{:S(2)}, u32[]{:S(2)}) collective-permute-start(f32[24,3,128]{2,1,0:T(4,128)S(1)} %get-tuple-element.164), channel_id=1, source_target_pairs={{0,3},{1,4},{2,5},{3,6},{4,7},{5,8},{6,9},{7,10},{8,11},{9,12},{10... | collective-permute-start | bytes 110600 | tf_op jit(solution)/shard_map/ppermute | solution.py:24
  143.0 12.1 %collective-permute-start.8 = (f32[24,3,128]{2,1,0:T(4,128)S(1)}, f32[24,3,128]{2,1,0:T(4,128)S(1)}, u32[]{:S(2)}, u32[]{:S(2)}) collective-permute-start(f32[24,3,128]{2,1,0:T(4,128)S(1)} %get-tuple-element.165), channel_id=1, source_target_pairs={{0,2},{1,3},{2,4},{3,5},{4,6},{5,7},{6,8},{7,9},{8,10},{9,11},{10,... | collective-permute-start | bytes 110600 | tf_op jit(solution)/shard_map/ppermute | solution.py:24
  149.2 15.9 %collective-permute-start.13 = (f32[24,16]{1,0:T(8,128)S(1)}, f32[24,16]{1,0:T(8,128)S(1)}, u32[]{:S(2)}, u32[]{:S(2)}) collective-permute-start(f32[24,16]{1,0:T(8,128)S(1)} %get-tuple-element.149), channel_id=1, source_target_pairs={{1,0},{2,1},{3,2},{4,3},{5,4},{6,5},{7,6},{8,7},{9,8},{10,9},{11,1... | collective-permute-start | bytes 4616 | tf_op jit(solution)/shard_map/ppermute | solution.py:18
  152.6 12.5 %collective-permute-start.12 = (f32[24,16]{1,0:T(8,128)S(1)}, f32[24,16]{1,0:T(8,128)S(1)}, u32[]{:S(2)}, u32[]{:S(2)}) collective-permute-start(f32[24,16]{1,0:T(8,128)S(1)} %get-tuple-element.149), channel_id=1, source_target_pairs={{0,1},{1,2},{2,3},{3,4},{4,5},{5,6},{6,7},{7,8},{8,9},{9,10},{10,1... | collective-permute-start | bytes 4616 | tf_op jit(solution)/shard_map/ppermute | solution.py:18
  155.2 10.5 %collective-permute-start.11 = (f32[24,7,128]{2,1,0:T(8,128)S(1)}, f32[24,7,128]{2,1,0:T(8,128)S(1)}, u32[]{:S(2)}, u32[]{:S(2)}) collective-permute-start(f32[24,7,128]{2,1,0:T(8,128)S(1)} %pad_maximum_fusion.7), channel_id=1, source_target_pairs={{1,0},{2,1},{3,2},{4,3},{5,4},{6,5},{7,6},{8,7},{9,8},{10,9},{11,1... | collective-permute-start | bytes 258056 | tf_op jit(solution)/shard_map/ppermute | solution.py:18
  163.2 11.7 %collective-permute-start.10 = (f32[24,7,128]{2,1,0:T(8,128)S(1)}, f32[24,7,128]{2,1,0:T(8,128)S(1)}, u32[]{:S(2)}, u32[]{:S(2)}) collective-permute-start(f32[24,7,128]{2,1,0:T(8,128)S(1)} %pad_maximum_fusion.7), channel_id=1, source_target_pairs={{0,1},{1,2},{2,3},{3,4},{4,5},{5,6},{6,7},{7,8},{8,9},{9,10},{10,1... | collective-permute-start | bytes 258056 | tf_op jit(solution)/shard_map/ppermute | solution.py:18
  175.7 12.7 %collective-permute-start.16 = (f32[24,4,128]{2,1,0:T(4,128)S(1)}, f32[24,4,128]{2,1,0:T(4,128)S(1)}, u32[]{:S(2)}, u32[]{:S(2)}) collective-permute-start(f32[24,4,128]{2,1,0:T(4,128)S(1)} %pad_maximum_fusion.10), channel_id=1, source_target_pairs={{0,1021},{1,1022},{2,1023},{3,0},{4,1},{5,2},{6,3},{7,4},{8,5},{9,... | collective-permute-start | bytes 147464 | tf_op jit(solution)/shard_map/ppermute | solution.py:24
  178.2 12.6 %collective-permute-start.15 = (f32[24,4,128]{2,1,0:T(4,128)S(1)}, f32[24,4,128]{2,1,0:T(4,128)S(1)}, u32[]{:S(2)}, u32[]{:S(2)}) collective-permute-start(f32[24,4,128]{2,1,0:T(4,128)S(1)} %pad_maximum_fusion.10), channel_id=1, source_target_pairs={{0,1022},{1,1023},{2,0},{3,1},{4,2},{5,3},{6,4},{7,5},{8,6},{9,7},... | collective-permute-start | bytes 147464 | tf_op jit(solution)/shard_map/ppermute | solution.py:24
  185.2 6.7 %collective-permute-start.14 = (f32[24,4,128]{2,1,0:T(4,128)S(1)}, f32[24,4,128]{2,1,0:T(4,128)S(1)}, u32[]{:S(2)}, u32[]{:S(2)}) collective-permute-start(f32[24,4,128]{2,1,0:T(4,128)S(1)} %pad_maximum_fusion.10), channel_id=1, source_target_pairs={{0,1023},{1,0},{2,1},{3,2},{4,3},{5,4},{6,5},{7,6},{8,7},{9,8},{10... | collective-permute-start | bytes 147464 | tf_op jit(solution)/shard_map/ppermute | solution.py:24
  270.1 13.3 %collective-permute-start.17 = (f32[24,3,128]{2,1,0:T(4,128)S(1)}, f32[24,3,128]{2,1,0:T(4,128)S(1)}, u32[]{:S(2)}, u32[]{:S(2)}) collective-permute-start(f32[24,3,128]{2,1,0:T(4,128)S(1)} %get-tuple-element.160), channel_id=1, source_target_pairs={{0,1},{1,2},{2,3},{3,4},{4,5},{5,6},{6,7},{7,8},{8,9},{9,10},{10,1... | collective-permute-start | bytes 110600 | tf_op jit(solution)/shard_map/ppermute | solution.py:24
  274.5 13.1 %collective-permute-start.19 = (f32[24,3,128]{2,1,0:T(4,128)S(1)}, f32[24,3,128]{2,1,0:T(4,128)S(1)}, u32[]{:S(2)}, u32[]{:S(2)}) collective-permute-start(f32[24,3,128]{2,1,0:T(4,128)S(1)} %get-tuple-element.161), channel_id=1, source_target_pairs={{0,3},{1,4},{2,5},{3,6},{4,7},{5,8},{6,9},{7,10},{8,11},{9,12},{10... | collective-permute-start | bytes 110600 | tf_op jit(solution)/shard_map/ppermute | solution.py:24
  280.8 12.3 %collective-permute-start.18 = (f32[24,3,128]{2,1,0:T(4,128)S(1)}, f32[24,3,128]{2,1,0:T(4,128)S(1)}, u32[]{:S(2)}, u32[]{:S(2)}) collective-permute-start(f32[24,3,128]{2,1,0:T(4,128)S(1)} %get-tuple-element.162), channel_id=1, source_target_pairs={{0,2},{1,3},{2,4},{3,5},{4,6},{5,7},{6,8},{7,9},{8,10},{9,11},{10,... | collective-permute-start | bytes 110600 | tf_op jit(solution)/shard_map/ppermute | solution.py:24
where the time goes:
time: 295 us; the launch traced here: 294 us
  other arithmetic  134 us (45%)
  starting transfers between devices  84 us (28%)
  local copies, waits for them, and re-layouts  29 us (10%)
  waiting for transfers between devices  26.1 us (9%)
  between operations  17.4 us (6%)
  loops' own time  2.99 us (1%)
    ppermute x12, starting transfers between devices, shifted_2(): return lax.ppermute(value, axis, pairs)  55.9 us
    reduce_sum x24, other arithmetic, pair_terms(): jnp.sum(kernel[:, :, None] * sources[:, :, 3][:, :, None, None, :] * sepa...  43.7 us
    scatter-add x24, other arithmetic, block_pass(): react_pool.at[source_ids.reshape(-1)]  40.6 us
    ppermute x8, starting transfers between devices, shifted(): lax.ppermute(value, axis, [(source, source + steps) for source in range(f...  28.1 us
    mul x24, other arithmetic, pair_terms(): kernel[:, :, None] * targets[:, 3][:, None, None, :, None] * separation  23.6 us
    reduce_sum x24, other arithmetic, pair_terms(): distance_sq = jnp.sum(separation * separation, axis=2) + soften  19.4 us
    ppermute x12, waiting for transfers between devices, shifted_2(): return lax.ppermute(value, axis, pairs)  17 us
    gather x24, local copies, waits for them, and re-layouts, block_pass(): jnp.take(tile_pool, source_ids, axis=0)  14.6 us
  transfers between devices with their start and end apart: 20, of which 6 were waited for; matrix products, arithmetic and copies ran while one was open for 2% of the time, Pallas kernels for 0%

commit v1 on v0

v1 whole, which is shorter than its diff:
```python
import functools

import jax
import jax.numpy as jnp
from jax import lax
from jax.experimental import pallas as pl
from jax.experimental.pallas import tpu as pltpu
from jax.sharding import PartitionSpec as P

STEPS = 2
soften = 0.05
time_step = 0.5

MESH = pl.DeviceIdType.MESH
F32 = jnp.float32
BF16 = jnp.bfloat16


def split_rows(rows):
    high = rows.astype(BF16)
    rest = rows - high.astype(F32)
    middle = rest.astype(BF16)
    low = rest - middle.astype(F32)
    return jnp.concatenate(
        [high.astype(F32), low, middle.astype(F32), jnp.zeros_like(low)], axis=0
    ).astype(BF16)


def fold(terms):
    return terms[:4] + terms[4:]


def kernel(
    dims, meta, part, first_out, second_out,
    first_pool, second_pool, terms, columns, self_act, act, react_all, react_out, react_in,
    rows_out, first_window, second_window, send, recv,
):
    outer, inner, tiles, listed, half = dims
    pools = (first_pool, second_pool)
    windows = (first_window, second_window)
    size = outer * inner
    reach = 2 * tiles
    slots = part.shape[2]
    zero_slot = tiles * listed
    inverse_at = tiles * listed
    occupancy_at = inverse_at + tiles * reach
    cuts_at = occupancy_at + tiles
    me = lax.axis_index("gx") * inner + lax.axis_index("gy")

    def device(distance):
        index = (me + distance + size) % size
        return (index // inner, index % inner)

    barrier = pltpu.get_barrier_semaphore()
    for distance in (-2, -1, 1, 2):
        pl.semaphore_signal(barrier, inc=1, device_id=device(distance), device_id_type=MESH)

    lanes = lax.broadcasted_iota(jnp.int32, (1, slots), 1)

    def weight_of(tile):
        return jnp.where(lanes < meta[occupancy_at + tile], 1.0, 0.0).astype(F32)

    for tile in range(tiles):
        first_pool[tile] = jnp.concatenate([part[tile, 0:3], weight_of(tile)], axis=0)
    react_all[zero_slot] = jnp.zeros((8, slots), F32)

    def remote(source, target, slot, distance):
        return pltpu.make_async_remote_copy(
            src_ref=source,
            dst_ref=target,
            send_sem=send.at[slot],
            recv_sem=recv.at[slot],
            device_id=device(distance),
            device_id_type=MESH,
        )

    def position_copies(step):
        return [
            remote(
                pools[step].at[pl.ds(0, tiles)],
                pools[step].at[pl.ds(tiles * distance, tiles)],
                6 * step + distance - 1,
                -distance,
            )
            for distance in (1, 2)
        ]

    def reaction_copies(step):
        return [
            remote(
                react_out.at[step, distance - 1],
                react_in.at[step, distance - 1],
                6 * step + 1 + distance,
                distance,
            )
            for distance in (1, 2)
        ]

    def window_copies(step):
        return [
            remote(
                rows_out.at[step, pl.ds(0, half)],
                windows[step].at[pl.ds(half + tiles, half)],
                6 * step + 4,
                -1,
            ),
            remote(
                rows_out.at[step, pl.ds(tiles - half, half)],
                windows[step].at[pl.ds(0, half)],
                6 * step + 5,
                1,
            ),
        ]

    def prepare(step, tile):
        rows = pools[step][tile]
        terms[tile] = split_rows(rows * rows[3:4])

    def pair(step, tile, source):
        rows = pools[step][source]
        dx = rows[0:1] - columns[tile, 0]
        dy = rows[1:2] - columns[tile, 1]
        dz = rows[2:3] - columns[tile, 2]
        root = lax.rsqrt(dx * dx + (dy * dy + (dz * dz + soften)))
        value = root * root * root
        high = value.astype(BF16)
        low = (value - high.astype(F32)).astype(BF16)
        return high, low

    def action_of(high, low, source):
        rows = terms[source]
        return lax.dot_general(
            jnp.concatenate([high, low], axis=1),
            jnp.concatenate([rows, rows], axis=1),
            (((1,), (1,)), ((), ())),
            preferred_element_type=F32,
        )

    def own_tile(step, tile):
        prepare(step, tile)
        rows = pools[step][tile]
        turned = jnp.transpose(jnp.concatenate([rows, rows], axis=0))
        for axis in range(3):
            columns[tile, axis] = jnp.broadcast_to(turned[:, axis : axis + 1], (slots, slots))
        high, low = pair(step, tile, tile)
        self_act[tile] = action_of(high, low, tile)

    def main_tile(step, tile):
        own = terms[tile]
        own_terms = jnp.concatenate([own, own], axis=1)
        total = self_act[tile]
        for entry in range(listed):
            source = meta[tile * listed + entry]
            high, low = pair(step, tile, source)
            total = total + action_of(high, low, source)
            reaction = jnp.dot(
                own_terms, jnp.concatenate([high, low], axis=0), preferred_element_type=F32
            )
            react_all[tile * listed + entry] = reaction[:8] + reaction[8:]
        turned = jnp.transpose(total)
        act[tile] = turned[:8] + turned[8:]

    def reactions_on(source):
        total = None
        for tile in range(max(0, source - reach), min(tiles, source)):
            entry = react_all[meta[inverse_at + tile * reach + source - tile - 1]]
            total = entry if total is None else total + entry
        return total

    for step in range(STEPS):
        if step == 0:
            pl.semaphore_wait(barrier, 4)
        positions = position_copies(step)
        for copy in positions:
            copy.start()

        lax.fori_loop(
            0, tiles, lambda tile, carry: (own_tile(step, tile), carry)[1], 0, unroll=4
        )
        for distance in (1, 2):
            positions[distance - 1].wait_recv()
            lax.fori_loop(
                tiles * distance,
                tiles * (distance + 1),
                lambda tile, carry: (prepare(step, tile), carry)[1],
                0,
                unroll=4,
            )
        lax.fori_loop(0, tiles, lambda tile, carry: (main_tile(step, tile), carry)[1], 0)

        reactions = reaction_copies(step)
        for distance in (2, 1):
            for tile in range(tiles):
                react_out[step, distance - 1, tile] = fold(
                    reactions_on(tiles * distance + tile)
                )
            reactions[distance - 1].start()
        for tile in range(1, tiles):
            act[tile] = act[tile] + reactions_on(tile)
        for distance in (1, 2):
            reactions[distance - 1].wait_recv()

        for tile in range(tiles):
            total = fold(act[tile]) + react_in[step, 0, tile] + react_in[step, 1, tile]
            rows = pools[step][tile]
            place, weight = rows[0:3], rows[3:4]
            speed = part[tile, 3:6] if step == 0 else rows_out[step - 1, tile, 3:6]
            acceleration = total[0:3] - place * total[3:4]
            speed = weight * (speed + (time_step / slots) * acceleration)
            place = weight * (place + time_step * speed)
            if step + 1 < STEPS:
                pools[step + 1][tile] = jnp.concatenate([place, weight], axis=0)
            rows_out[step, tile] = jnp.concatenate([place, speed], axis=0)
            windows[step][half + tile] = jnp.concatenate([place, speed], axis=0)
        for copy in window_copies(step):
            copy.start()

    for step, out in enumerate((first_out, second_out)):
        for copy in window_copies(step):
            copy.wait_recv()
        begin = meta[cuts_at + 2 * step]
        count = meta[cuts_at + 2 * step + 1]
        for slot in range(2 * tiles):
            rows = windows[step][jnp.minimum(begin + slot, 2 * tiles - 1)]
            out[slot] = jnp.where(slot < count, rows, 0.0)
    for step in range(STEPS):
        for copy in position_copies(step) + reaction_copies(step) + window_copies(step):
            copy.wait_send()


def body(outer, inner, particles, occupancy, neighbours, curve_cuts):
    tiles, fields, slots = particles.shape
    listed = neighbours.shape[1]
    size = outer * inner
    total = size * tiles
    reach = 2 * tiles
    half = tiles // 2
    me = lax.axis_index(("gx", "gy"))
    first = me * tiles
    local = (neighbours - first) % total
    tile_ids = jnp.arange(tiles, dtype=jnp.int32)
    entry_ids = jnp.arange(tiles * listed, dtype=jnp.int32).reshape(tiles, listed)
    offsets = jnp.arange(1, reach + 1, dtype=jnp.int32)
    hit = (local - tile_ids[:, None])[:, None, :] == offsets[None, :, None]
    none = tiles * listed
    inverse = none + jnp.sum(jnp.where(hit, entry_ids[:, None, :] - none, 0), axis=2)
    starts = curve_cuts[:, me]
    ends = jnp.where(me + 1 < size, curve_cuts[:, jnp.minimum(me + 1, size - 1)], total)
    cuts = jnp.stack([starts - (first - half), ends - starts], axis=1)
    meta = jnp.concatenate(
        [local.reshape(-1), inverse.reshape(-1), occupancy, cuts.reshape(-1)]
    ).astype(jnp.int32)
    out_type = jax.ShapeDtypeStruct((2 * tiles, fields, slots), F32)
    vmem = pl.BlockSpec(memory_space=pltpu.VMEM)
    return pl.pallas_call(
        functools.partial(kernel, (outer, inner, tiles, listed, half)),
        out_shape=(out_type, out_type),
        in_specs=[pl.BlockSpec(memory_space=pltpu.SMEM), vmem],
        out_specs=(vmem, vmem),
        scratch_shapes=[
            pltpu.VMEM((3 * tiles, 4, slots), F32),
            pltpu.VMEM((3 * tiles, 4, slots), F32),
            pltpu.VMEM((3 * tiles, 16, slots), BF16),
            pltpu.VMEM((tiles, 3, slots, slots), F32),
            pltpu.VMEM((tiles, slots, 16), F32),
            pltpu.VMEM((tiles, 8, slots), F32),
            pltpu.VMEM((tiles * listed + 1, 8, slots), F32),
            pltpu.VMEM((STEPS, 2, tiles, 4, slots), F32),
            pltpu.VMEM((STEPS, 2, tiles, 4, slots), F32),
            pltpu.VMEM((STEPS, tiles, fields, slots), F32),
            pltpu.VMEM((2 * tiles, fields, slots), F32),
            pltpu.VMEM((2 * tiles, fields, slots), F32),
            pltpu.SemaphoreType.DMA((6 * STEPS,)),
            pltpu.SemaphoreType.DMA((6 * STEPS,)),
        ],
        compiler_params=pltpu.CompilerParams(
            collective_id=0, has_side_effects=True, vmem_limit_bytes=40 << 20
        ),
    )(meta, particles)


def solution(mesh):
    in_specs = (P(("gx", "gy"), None, None), P(("gx", "gy")), P(("gx", "gy"), None), P())
    out_specs = (P(("gx", "gy"), None, None), P(("gx", "gy"), None, None))
    per_device = functools.partial(body, mesh.shape["gx"], mesh.shape["gy"])
    return jax.shard_map(
        per_device, mesh=mesh, in_specs=in_specs, out_specs=out_specs, check_vma=False
    )
```

time: 295 us -> 69.9 us (0.24)
  the two profiles are of different devices: /device:TPU:514 before, /device:TPU:2 now
where the time goes in v1:
time: 69.9 us; the launch traced here: 69.7 us
  Pallas kernels  65.8 us (94%)
  local copies, waits for them, and re-layouts  2.12 us (3%)
  other arithmetic  1.14 us (2%)
    pallas_call x1, Pallas kernels, body(): pl.pallas_call(functools.partial(kernel, (outer, inner, tiles, listed, ha...  65.8 us

profile of v1, /device:TPU:2, one launch (start us, length us, event | category | flops | bytes accessed | tf_op | source)
XLA Modules:
  0.0 69.7 jit_solution(8827177439728383563)
XLA Ops:
  0.6 0.0 copy-start.1
  0.7 0.8 %dynamic-slice_subtract_fusion = (s32[2,1]{1,0:T(2,128)S(1)}, s32[2,1]{1,0:T(2,128)S(1)}) fusion(s32[2,1024]{1,0:T(2,128)} %param.7, s32[]{:T(128)S(6)} %select_n.28, s32[]{:T(128)S(6)} %sub.37, s32[]{:T(128)S(6)} %select_n.30, pred[]{:T(512)S(6)} %lt.17), kind=kLoop, calls=%fused_computation.9 | loop fusion | flops 6 | bytes 45 | tf_op jit(solution)/shard_map/sub | solution.py:249
  1.5 0.1 pad_add_fusion.1
  1.6 0.1 reshape.35
  1.6 0.0 copy-done.1
  1.7 0.0 copy-start
  1.7 0.1 select_reduce_fusion
  1.8 0.1 add.57
  1.9 0.0 copy-start.2
  1.9 0.1 reshape.34
  2.0 0.6 copy-done.2
  2.6 0.1 pad_add_fusion.meta
  2.6 0.0 copy-done
  2.6 65.8 %shard_map.59 = (f32[24,6,128]{2,1,0:T(8,128)S(1)}, f32[24,6,128]{2,1,0:T(8,128)S(1)}) custom-call(s32[496]{0:T(512)S(1)} %pad_add_fusion.meta, f32[12,6,128]{2,1,0:T(8,128)S(1)} %copy-done), custom_call_target="tpu_custom_call" | custom-call | tf_op jit(solution)/shard_map/pallas_call | solution.py:255
  68.4 0.6 copy.8
  69.1 0.6 copy.9
  (3 shorter events, 0.0 us)
Async XLA Ops:
  0.6 1.0 %copy-start.1 = (s32[12,16]{1,0:T(8,128)S(1)}, s32[12,16]{1,0:T(8,128)}, u32[]{:S(2)}) copy-start(s32[12,16]{1,0:T(8,128)} %param.6) | copy-start | bytes 2308
  1.7 1.0 %copy-start = (f32[12,6,128]{2,1,0:T(8,128)S(1)}, f32[12,6,128]{2,1,0:T(8,128)}, u32[]{:S(2)}) copy-start(f32[12,6,128]{2,1,0:T(8,128)} %part.1) | copy-start | bytes 110596
  1.9 0.7 copy-start.2

commit v2 on v1

v2 whole, which is shorter than its diff:
```python
import functools

import jax
import jax.numpy as jnp
from jax import lax
from jax.experimental import pallas as pl
from jax.experimental.pallas import tpu as pltpu
from jax.sharding import PartitionSpec as P

STEPS = 2
soften = 0.05
time_step = 0.5

MESH = pl.DeviceIdType.MESH
F32 = jnp.float32
BF16 = jnp.bfloat16


def split_rows(rows):
    high = rows.astype(BF16)
    rest = rows - high.astype(F32)
    middle = rest.astype(BF16)
    low = rest - middle.astype(F32)
    return jnp.concatenate(
        [high.astype(F32), low, middle.astype(F32), jnp.zeros_like(low)], axis=0
    ).astype(BF16)


def fold(terms):
    return terms[:4] + terms[4:]


def kernel(
    dims, neighbours, inverse, occupancy, cuts, part, first_out, second_out,
    first_pool, second_pool, speeds, state, terms, columns, self_act, act, react_all,
    partial, from_next, from_second_next, from_last, from_second_last,
    end_last, end_next, end_second_last, end_third_last, first_window, second_window,
    send, recv,
):
    outer, inner, tiles, listed, half = dims
    pools = (first_pool, second_pool)
    size = outer * inner
    total_tiles = size * tiles
    reach = 2 * tiles
    slots = part.shape[2]
    zero_slot = tiles * listed
    me = lax.axis_index("gx") * inner + lax.axis_index("gy")
    first = me * tiles

    def device(distance):
        index = (me + distance + size) % size
        return (index // inner, index % inner)

    barrier = pltpu.get_barrier_semaphore()
    for distance in (-1, 1, -2, 2, -3, 3):
        pl.semaphore_signal(barrier, inc=1, device_id=device(distance), device_id_type=MESH)

    lanes = lax.broadcasted_iota(jnp.int32, (1, slots), 1)
    empty = jnp.zeros((1, slots), F32)
    for tile in range(tiles):
        weight = jnp.where(lanes < occupancy[tile], 1.0, 0.0).astype(F32)
        first_pool[tile] = jnp.concatenate([part[tile, 0:3], weight], axis=0)
        speeds[tile] = jnp.concatenate([part[tile, 3:6], empty], axis=0)
    react_all[zero_slot] = jnp.zeros((8, slots), F32)

    def remote(source, target, slot, distance):
        return pltpu.make_async_remote_copy(
            src_ref=source,
            dst_ref=target,
            send_sem=send.at[slot],
            recv_sem=recv.at[slot],
            device_id=device(distance),
            device_id_type=MESH,
        )

    def tile_copies(buffer, slot):
        return [
            remote(
                buffer.at[pl.ds(0, tiles)],
                buffer.at[pl.ds(tiles * distance, tiles)],
                slot + distance - 1,
                -distance,
            )
            for distance in (1, 2)
        ]

    def rows_copy(step, begin, count, target, slot, distance):
        return remote(partial.at[step, pl.ds(begin, count)], target, slot, distance)

    positions = tile_copies(first_pool, 0)
    motions = tile_copies(speeds, 2)
    mid = [
        rows_copy(0, tiles, 2 * tiles, from_last, 4, 1),
        rows_copy(0, 2 * tiles, tiles, from_second_last, 5, 2),
        rows_copy(0, 0, tiles, from_second_next, 6, -2),
        rows_copy(0, 0, 2 * tiles, from_next, 7, -1),
    ]
    border = remote(
        state.at[pl.ds(tiles - half, half)], state.at[pl.ds(3 * tiles, half)], 8, 1
    )
    end = [
        rows_copy(1, 2 * tiles + half, half, end_third_last, 9, 3),
        rows_copy(1, tiles + half, tiles + half, end_second_last, 10, 2),
        rows_copy(1, half, 2 * tiles, end_last, 11, 1),
        rows_copy(1, 0, half, end_next, 12, -1),
    ]

    def over(begin, end, function, unroll):
        def trip(tile, carry):
            function(tile)
            return carry

        lax.fori_loop(begin, end, trip, 0, unroll=unroll)

    def prepare(rows, tile):
        terms[tile] = split_rows(rows * rows[3:4])

    def pair(step, tile, source):
        rows = pools[step][source]
        dx = rows[0:1] - columns[tile, 0]
        dy = rows[1:2] - columns[tile, 1]
        dz = rows[2:3] - columns[tile, 2]
        root = lax.rsqrt(dx * dx + (dy * dy + (dz * dz + soften)))
        value = root * root * root
        high = value.astype(BF16)
        low = (value - high.astype(F32)).astype(BF16)
        return high, low

    def action_of(high, low, source):
        rows = terms[source]
        return lax.dot_general(
            jnp.concatenate([high, low], axis=1),
            jnp.concatenate([rows, rows], axis=1),
            (((1,), (1,)), ((), ())),
            preferred_element_type=F32,
        )

    def own_tile(step, tile):
        rows = pools[step][tile]
        prepare(rows, tile)
        turned = jnp.transpose(jnp.concatenate([rows, rows], axis=0))
        for axis in range(3):
            columns[tile, axis] = jnp.broadcast_to(turned[:, axis : axis + 1], (slots, slots))
        high, low = pair(step, tile, tile)
        self_act[tile] = action_of(high, low, tile)

    def main_tile(step, tile):
        own = terms[tile]
        own_terms = jnp.concatenate([own, own], axis=1)
        total = self_act[tile]
        for entry in range(listed):
            source = jnp.minimum(
                lax.rem(neighbours[tile, entry] - first + total_tiles, total_tiles),
                3 * tiles - 1,
            )
            high, low = pair(step, tile, source)
            total = total + action_of(high, low, source)
            reaction = jnp.dot(
                own_terms, jnp.concatenate([high, low], axis=0), preferred_element_type=F32
            )
            react_all[tile * listed + entry] = reaction[:8] + reaction[8:]
        turned = jnp.transpose(total)
        act[tile] = turned[:8] + turned[8:]

    def reactions_on(source):
        total = None
        for tile in range(max(0, source - reach), min(tiles, source)):
            entry = react_all[inverse[tile, source - tile - 1]]
            total = entry if total is None else total + entry
        return total

    def moved(place, speed, weight, total):
        acceleration = total[0:3] - place * total[3:4]
        speed = weight * (speed + (time_step / slots) * acceleration)
        place = weight * (place + time_step * speed)
        return place, speed

    pl.semaphore_wait(barrier, 6)
    for copy in positions + motions:
        copy.start()
    over(0, tiles, lambda tile: own_tile(0, tile), 4)
    for distance in (1, 2):
        positions[distance - 1].wait_recv()
        over(
            tiles * distance,
            tiles * (distance + 1),
            lambda tile: prepare(first_pool[tile], tile),
            4,
        )
    over(0, tiles, lambda tile: main_tile(0, tile), 1)

    for tile in range(2 * tiles, 3 * tiles):
        partial[0, tile] = fold(reactions_on(tile))
    mid[1].start()
    for tile in range(tiles, 2 * tiles):
        partial[0, tile] = fold(reactions_on(tile))
    mid[0].start()
    for tile in range(tiles):
        total = act[tile] if tile == 0 else act[tile] + reactions_on(tile)
        partial[0, tile] = fold(total)
    mid[2].start()
    mid[3].start()

    def first_update(tile, total):
        rows, speed = first_pool[tile], speeds[tile]
        place, speed = moved(rows[0:3], speed[0:3], rows[3:4], total)
        second_pool[tile] = jnp.concatenate([place, rows[3:4]], axis=0)
        state[tile] = jnp.concatenate([place, speed, rows[3:4], empty], axis=0)

    mid[0].wait_recv()
    mid[1].wait_recv()
    over(
        0,
        tiles,
        lambda tile: first_update(
            tile, partial[0, tile] + from_last[tile] + from_second_last[tile]
        ),
        4,
    )
    border.start()
    over(0, tiles, lambda tile: own_tile(1, tile), 4)
    motions[0].wait_recv()
    motions[1].wait_recv()
    mid[3].wait_recv()

    def next_update(tile):
        first_update(
            tiles + tile, from_next[tile] + partial[0, tiles + tile] + from_last[tiles + tile]
        )
        prepare(second_pool[tiles + tile], tiles + tile)

    over(0, tiles, next_update, 4)
    mid[2].wait_recv()

    def second_next_update(tile):
        first_update(
            2 * tiles + tile,
            from_second_next[tile] + from_next[tiles + tile] + partial[0, 2 * tiles + tile],
        )
        prepare(second_pool[2 * tiles + tile], 2 * tiles + tile)

    over(0, tiles, second_next_update, 4)
    over(0, tiles, lambda tile: main_tile(1, tile), 1)

    for tile in range(2 * tiles, 3 * tiles):
        partial[1, tile] = fold(reactions_on(tile))
    end[0].start()
    for tile in range(tiles, 2 * tiles):
        partial[1, tile] = fold(reactions_on(tile))
    end[1].start()
    for tile in range(tiles):
        total = act[tile] if tile == 0 else act[tile] + reactions_on(tile)
        partial[1, tile] = fold(total)
    end[2].start()
    end[3].start()

    border.wait_recv()
    for tile in range(half):
        first_window[tile] = state[3 * tiles + tile, 0:6]
    for tile in range(tiles + half):
        first_window[half + tile] = state[tile, 0:6]

    def place_slots(step, window, out):
        begin = cuts[step, me] - (first - half)
        following = cuts[step, jnp.minimum(me + 1, size - 1)]
        count = jnp.where(me + 1 < size, following, total_tiles) - cuts[step, me]
        for slot in range(2 * tiles):
            rows = window[jnp.clip(begin + slot, 0, 2 * tiles - 1)]
            out[slot] = jnp.where(slot < count, rows, 0.0)

    place_slots(0, first_window, first_out)

    def second_update(tile, slot, total):
        rows = state[tile]
        place, speed = moved(rows[0:3], rows[3:6], rows[6:7], total)
        second_window[slot] = jnp.concatenate([place, speed], axis=0)

    end[2].wait_recv()
    end[1].wait_recv()
    for tile in range(tiles):
        second_update(
            tile,
            half + tile,
            partial[1, tile] + end_last[half + tile] + end_second_last[half + tile],
        )
    end[3].wait_recv()
    for tile in range(half):
        second_update(
            tiles + tile,
            half + tiles + tile,
            end_next[tile] + partial[1, tiles + tile] + end_last[tiles + half + tile],
        )
    end[0].wait_recv()
    for tile in range(half):
        second_update(
            3 * tiles + tile, tile, end_last[tile] + end_second_last[tile] + end_third_last[tile]
        )
    place_slots(1, second_window, second_out)
    for copy in positions + motions + mid + [border] + end:
        copy.wait_send()


def body(outer, inner, particles, occupancy, neighbours, curve_cuts):
    tiles, fields, slots = particles.shape
    listed = neighbours.shape[1]
    total = outer * inner * tiles
    reach = 2 * tiles
    half = tiles // 2
    first = lax.axis_index(("gx", "gy")) * tiles
    tile_ids = jnp.arange(tiles, dtype=jnp.int32)
    offset = (neighbours - (first + tile_ids)[:, None]) % total
    entry_ids = jnp.arange(tiles * listed, dtype=jnp.int32).reshape(tiles, listed)
    offsets = jnp.arange(1, reach + 1, dtype=jnp.int32)
    hit = offset[:, None, :] == offsets[None, :, None]
    none = tiles * listed
    inverse = none + jnp.sum(jnp.where(hit, entry_ids[:, None, :] - none, 0), axis=2)
    out_type = jax.ShapeDtypeStruct((2 * tiles, fields, slots), F32)
    vmem = pl.BlockSpec(memory_space=pltpu.VMEM)
    smem = pl.BlockSpec(memory_space=pltpu.SMEM)

    def rows(*extent):
        return pltpu.VMEM(extent + (slots,), F32)

    return pl.pallas_call(
        functools.partial(kernel, (outer, inner, tiles, listed, half)),
        out_shape=(out_type, out_type),
        in_specs=[smem, smem, smem, smem, vmem],
        out_specs=(vmem, vmem),
        scratch_shapes=[
            rows(3 * tiles, 4),
            rows(3 * tiles, 4),
            rows(3 * tiles, 4),
            rows(3 * tiles + half, 8),
            pltpu.VMEM((3 * tiles, 16, slots), BF16),
            rows(tiles, 3, slots),
            pltpu.VMEM((tiles, slots, 16), F32),
            rows(tiles, 8),
            rows(tiles * listed + 1, 8),
            rows(STEPS, 3 * tiles, 4),
            rows(2 * tiles, 4),
            rows(tiles, 4),
            rows(2 * tiles, 4),
            rows(tiles, 4),
            rows(2 * tiles, 4),
            rows(half, 4),
            rows(tiles + half, 4),
            rows(half, 4),
            rows(2 * tiles, fields),
            rows(2 * tiles, fields),
            pltpu.SemaphoreType.DMA((13,)),
            pltpu.SemaphoreType.DMA((13,)),
        ],
        compiler_params=pltpu.CompilerParams(
            collective_id=0, has_side_effects=True, vmem_limit_bytes=40 << 20
        ),
    )(neighbours, inverse, occupancy, curve_cuts, particles)


def solution(mesh):
    in_specs = (P(("gx", "gy"), None, None), P(("gx", "gy")), P(("gx", "gy"), None), P())
    out_specs = (P(("gx", "gy"), None, None), P(("gx", "gy"), None, None))
    per_device = functools.partial(body, mesh.shape["gx"], mesh.shape["gy"])
    return jax.shard_map(
        per_device, mesh=mesh, in_specs=in_specs, out_specs=out_specs, check_vma=False
    )
```

time: 69.9 us -> 63.4 us (0.907)
  Pallas kernels: 65.8 us -> 59.7 us
  other arithmetic: 1.14 us -> 0.22 us
    pallas_call x1, Pallas kernels: 65.8 us -> 59.7 us  [body(): pl.pallas_call(functools.partial(kernel, (outer, inner, tiles, listed, ha...]
    sub x2 -> x0, other arithmetic: 0.85 us -> none  [the longest x1 0.83 us: body(): cuts = jnp.stack([starts - (first - half), ends - starts], axis=1)]
    unnamed x6 -> x8, local copies, waits for them, and re-layouts: 0.58 us -> 1.32 us
where the time goes in v2:
time: 63.4 us; the launch traced here: 63.2 us
  Pallas kernels  59.7 us (94%)
  local copies, waits for them, and re-layouts  2.62 us (4%)
  between operations  0.71 us (1%)
    pallas_call x1, Pallas kernels, body(): pl.pallas_call(functools.partial(kernel, (outer, inner, tiles, listed, ha...  59.7 us
    unnamed x8, local copies, waits for them, and re-layouts  1.32 us
    pallas_call x2, local copies, waits for them, and re-layouts, body(): pl.pallas_call(functools.partial(kernel, (outer, inner, tiles, listed, ha...  1.29 us

profile of v2, /device:TPU:2, one launch (start us, length us, event | category | flops | bytes accessed | tf_op | source)
XLA Modules:
  0.0 63.2 jit_solution(14416501670999262102)
XLA Ops:
  0.6 0.0 copy-start.1
  0.6 0.0 copy-start
  0.7 0.7 %copy-done.1 = s32[12,16]{1,0:T(8,128)S(1)} copy-done((s32[12,16]{1,0:T(8,128)S(1)}, s32[12,16]{1,0:T(8,128)}, u32[]{:S(2)}) %copy-start.1) | copy-done | bytes 792
  1.3 0.1 add_select_fusion
  1.4 0.1 select_reduce_fusion
  1.5 0.0 copy-start.2
  1.6 0.0 copy-start.3
  1.6 0.0 copy-done
  1.6 0.7 %copy-done.2 = s32[2,1024]{1,0:T(2,128)S(1)} copy-done((s32[2,1024]{1,0:T(2,128)S(1)}, s32[2,1024]{1,0:T(2,128)}, u32[]{:S(2)}) %copy-start.2) | copy-done | bytes 8216
  2.2 0.0 copy-done.3
  2.2 59.7 %shard_map.59 = (f32[24,6,128]{2,1,0:T(8,128)S(1)}, f32[24,6,128]{2,1,0:T(8,128)S(1)}) custom-call(s32[12,16]{1,0:T(8,128)S(1)} %copy-done.1, s32[12,24]{1,0:T(8,128)S(1)} %broadcast_add_fusion.inverse, s32[12]{0:T(128)S(1)} %copy-done.3, s32[2,1024]{1,0:T(2,128)S(1)} %copy-done.2, f32[12,6,128]{2,1,0:T(8,128)S(1)} %copy-done), custom_call_target="tpu_custom_call" | custom-call | tf_op jit(solution)/shard_map/pallas_call | solution.py:324
  61.9 0.6 %copy.8 = f32[24,6,128]{2,0,1:T(8,128)} copy(f32[24,6,128]{2,1,0:T(8,128)S(1)} %get-tuple-element.4) | data formatting | bytes 147456 | tf_op jit(solution)/shard_map/pallas_call | solution.py:324
  62.6 0.6 %copy.9 = f32[24,6,128]{2,0,1:T(8,128)} copy(f32[24,6,128]{2,1,0:T(8,128)S(1)} %get-tuple-element.5) | data formatting | bytes 147456 | tf_op jit(solution)/shard_map/pallas_call | solution.py:324
  (3 shorter events, 0.0 us)
Async XLA Ops:
  0.6 0.7 %copy-start.1 = (s32[12,16]{1,0:T(8,128)S(1)}, s32[12,16]{1,0:T(8,128)}, u32[]{:S(2)}) copy-start(s32[12,16]{1,0:T(8,128)} %neighbours.1) | copy-start | bytes 2308
  0.6 0.9 %copy-start = (f32[12,6,128]{2,1,0:T(8,128)S(1)}, f32[12,6,128]{2,1,0:T(8,128)}, u32[]{:S(2)}) copy-start(f32[12,6,128]{2,1,0:T(8,128)} %part.1) | copy-start | bytes 110596
  1.5 0.7 %copy-start.2 = (s32[2,1024]{1,0:T(2,128)S(1)}, s32[2,1024]{1,0:T(2,128)}, u32[]{:S(2)}) copy-start(s32[2,1024]{1,0:T(2,128)} %cuts.1) | copy-start | bytes 24580
  1.6 0.7 %copy-start.3 = (s32[12]{0:T(128)S(1)}, s32[12]{0:T(128)}, u32[]{:S(2)}) copy-start(s32[12]{0:T(128)} %occupancy.1) | copy-start | bytes 148

commit v3 on v2

--- a/solution.py
+++ b/solution.py
@@ -31,18 +31,19 @@
 
 
 def kernel(
-    dims, neighbours, inverse, occupancy, cuts, part, first_out, second_out,
+    dims, neighbours_far, occupancy_far, cuts_far, part_far, first_out, second_out,
     first_pool, second_pool, speeds, state, terms, columns, self_act, act, react_all,
     partial, from_next, from_second_next, from_last, from_second_last,
     end_last, end_next, end_second_last, end_third_last, first_window, second_window,
-    send, recv,
+    neighbours, neighbour_rows, occupancy, cuts, part, inverse_rows, inverse,
+    send, recv, near,
 ):
     outer, inner, tiles, listed, half = dims
     pools = (first_pool, second_pool)
     size = outer * inner
     total_tiles = size * tiles
     reach = 2 * tiles
-    slots = part.shape[2]
+    slots = part_far.shape[2]
     zero_slot = tiles * listed
     me = lax.axis_index("gx") * inner + lax.axis_index("gy")
     first = me * tiles
@@ -55,13 +56,45 @@
     for distance in (-1, 1, -2, 2, -3, 3):
         pl.semaphore_signal(barrier, inc=1, device_id=device(distance), device_id_type=MESH)
 
+    loads = [
+        pltpu.make_async_copy(source, target, near.at[slot])
+        for slot, (source, target) in enumerate(
+            (
+                (occupancy_far, occupancy),
+                (part_far, part),
+                (neighbours_far, neighbour_rows),
+                (neighbours_far, neighbours),
+                (cuts_far, cuts),
+            ),
+            1,
+        )
+    ]
+    for load in loads:
+        load.start()
+    react_all[zero_slot] = jnp.zeros((8, slots), F32)
+    inverse_copy = pltpu.make_async_copy(inverse_rows, inverse, near.at[0])
+
+    def find_entries():
+        own_id = lax.broadcasted_iota(jnp.int32, (tiles, listed), 0)
+        entry_id = lax.broadcasted_iota(jnp.int32, (tiles, listed), 1)
+        offset = neighbour_rows[...] - first - own_id
+        offset = jnp.where(offset < 0, offset + total_tiles, offset)
+        mark = own_id * listed + entry_id - zero_slot
+        place = lax.broadcasted_iota(jnp.int32, (tiles, reach), 1)
+        found = jnp.full((tiles, reach), zero_slot, jnp.int32)
+        for distance in range(1, reach + 1):
+            entry = jnp.sum(jnp.where(offset == distance, mark, 0), axis=1, keepdims=True)
+            found = found + jnp.where(place == distance - 1, entry, 0)
+        inverse_rows[...] = jnp.clip(found, 0, zero_slot)
+
+    for load in loads:
+        load.wait()
     lanes = lax.broadcasted_iota(jnp.int32, (1, slots), 1)
     empty = jnp.zeros((1, slots), F32)
     for tile in range(tiles):
         weight = jnp.where(lanes < occupancy[tile], 1.0, 0.0).astype(F32)
         first_pool[tile] = jnp.concatenate([part[tile, 0:3], weight], axis=0)
         speeds[tile] = jnp.concatenate([part[tile, 3:6], empty], axis=0)
-    react_all[zero_slot] = jnp.zeros((8, slots), F32)
 
     def remote(source, target, slot, distance):
         return pltpu.make_async_remote_copy(
@@ -175,9 +208,11 @@
         place = weight * (place + time_step * speed)
         return place, speed
 
+    find_entries()
     pl.semaphore_wait(barrier, 6)
     for copy in positions + motions:
         copy.start()
+    inverse_copy.start()
     over(0, tiles, lambda tile: own_tile(0, tile), 4)
     for distance in (1, 2):
         positions[distance - 1].wait_recv()
@@ -188,6 +223,7 @@
             4,
         )
     over(0, tiles, lambda tile: main_tile(0, tile), 1)
+    inverse_copy.wait()
 
     for tile in range(2 * tiles, 3 * tiles):
         partial[0, tile] = fold(reactions_on(tile))
@@ -266,7 +302,7 @@
         count = jnp.where(me + 1 < size, following, total_tiles) - cuts[step, me]
         for slot in range(2 * tiles):
             rows = window[jnp.clip(begin + slot, 0, 2 * tiles - 1)]
-            out[slot] = jnp.where(slot < count, rows, 0.0)
+            out[:, slot, :] = jnp.where(slot < count, rows, 0.0)
 
     place_slots(0, first_window, first_out)
 
@@ -303,57 +339,61 @@
 def body(outer, inner, particles, occupancy, neighbours, curve_cuts):
     tiles, fields, slots = particles.shape
     listed = neighbours.shape[1]
-    total = outer * inner * tiles
-    reach = 2 * tiles
     half = tiles // 2
-    first = lax.axis_index(("gx", "gy")) * tiles
-    tile_ids = jnp.arange(tiles, dtype=jnp.int32)
-    offset = (neighbours - (first + tile_ids)[:, None]) % total
-    entry_ids = jnp.arange(tiles * listed, dtype=jnp.int32).reshape(tiles, listed)
-    offsets = jnp.arange(1, reach + 1, dtype=jnp.int32)
-    hit = offset[:, None, :] == offsets[None, :, None]
-    none = tiles * listed
-    inverse = none + jnp.sum(jnp.where(hit, entry_ids[:, None, :] - none, 0), axis=2)
-    out_type = jax.ShapeDtypeStruct((2 * tiles, fields, slots), F32)
+    out_type = jax.ShapeDtypeStruct((fields, 2 * tiles, slots), F32)
     vmem = pl.BlockSpec(memory_space=pltpu.VMEM)
-    smem = pl.BlockSpec(memory_space=pltpu.SMEM)
-
-    def rows(*extent):
+    far = pl.BlockSpec(memory_space=pltpu.MemorySpace.HBM)
+
+    def held(*extent):
         return pltpu.VMEM(extent + (slots,), F32)
 
-    return pl.pallas_call(
+    outputs = pl.pallas_call(
         functools.partial(kernel, (outer, inner, tiles, listed, half)),
         out_shape=(out_type, out_type),
-        in_specs=[smem, smem, smem, smem, vmem],
+        in_specs=[far] * 4,
         out_specs=(vmem, vmem),
         scratch_shapes=[
-            rows(3 * tiles, 4),
-            rows(3 * tiles, 4),
-            rows(3 * tiles, 4),
-            rows(3 * tiles + half, 8),
+            held(3 * tiles, 4),
+            held(3 * tiles, 4),
+            held(3 * tiles, 4),
+            held(3 * tiles + half, 8),
             pltpu.VMEM((3 * tiles, 16, slots), BF16),
-            rows(tiles, 3, slots),
+            held(tiles, 3, slots),
             pltpu.VMEM((tiles, slots, 16), F32),
-            rows(tiles, 8),
-            rows(tiles * listed + 1, 8),
-            rows(STEPS, 3 * tiles, 4),
-            rows(2 * tiles, 4),
-            rows(tiles, 4),
-            rows(2 * tiles, 4),
-            rows(tiles, 4),
-            rows(2 * tiles, 4),
-            rows(half, 4),
-            rows(tiles + half, 4),
-            rows(half, 4),
-            rows(2 * tiles, fields),
-            rows(2 * tiles, fields),
+            held(tiles, 8),
+            held(tiles * listed + 1, 8),
+            held(STEPS, 3 * tiles, 4),
+            held(2 * tiles, 4),
+            held(tiles, 4),
+            held(2 * tiles, 4),
+            held(tiles, 4),
+            held(2 * tiles, 4),
+            held(half, 4),
+            held(tiles + half, 4),
+            held(half, 4),
+            held(2 * tiles, fields),
+            held(2 * tiles, fields),
+            pltpu.SMEM(neighbours.shape, jnp.int32),
+            pltpu.VMEM(neighbours.shape, jnp.int32),
+            pltpu.SMEM(occupancy.shape, jnp.int32),
+            pltpu.SMEM(curve_cuts.shape, jnp.int32),
+            pltpu.VMEM(particles.shape, F32),
+            pltpu.VMEM((tiles, 2 * tiles), jnp.int32),
+            pltpu.SMEM((tiles, 2 * tiles), jnp.int32),
             pltpu.SemaphoreType.DMA((13,)),
             pltpu.SemaphoreType.DMA((13,)),
+            pltpu.SemaphoreType.DMA((6,)),
         ],
         compiler_params=pltpu.CompilerParams(
             collective_id=0, has_side_effects=True, vmem_limit_bytes=40 << 20
         ),
-    )(neighbours, inverse, occupancy, curve_cuts, particles)
+    )(
+        *(
+            pltpu.with_memory_space_constraint(operand, pltpu.MemorySpace.HBM)
+            for operand in (neighbours, occupancy, curve_cuts, particles)
+        )
+    )
+    return tuple(jnp.transpose(rows, (1, 0, 2)) for rows in outputs)
 
 
 def solution(mesh):

time: 63.4 us -> 61 us (0.962)
  local copies, waits for them, and re-layouts: 2.62 us -> 1.27 us
  Pallas kernels: 59.7 us -> 58.8 us
    pallas_call x2 -> x0, local copies, waits for them, and re-layouts: 1.29 us -> none  [body(): pl.pallas_call(functools.partial(kernel, (outer, inner, tiles, listed, ha...]
    pallas_call x1, Pallas kernels: 59.7 us -> 58.8 us  [body(): pl.pallas_call(functools.partial(kernel, (outer, inner, tiles, listed, ha...]
    unnamed x8 -> x2, local copies, waits for them, and re-layouts: 1.32 us -> 1.27 us
where the time goes in v3:
time: 61 us; the launch traced here: 60.7 us
  Pallas kernels  58.8 us (96%)
  local copies, waits for them, and re-layouts  1.27 us (2%)
  between operations  0.64 us (1%)
    pallas_call x1, Pallas kernels, body(): pl.pallas_call(functools.partial(kernel, (outer, inner, tiles, listed, ha...  58.8 us
    unnamed x2, local copies, waits for them, and re-layouts  1.27 us

profile of v3, /device:TPU:2, one launch (start us, length us, event | category | flops | bytes accessed | tf_op | source)
XLA Modules:
  0.0 60.7 jit_solution(190155930061887854)
XLA Ops:
  0.6 58.8 %shard_map.59 = (f32[6,24,128]{2,1,0:T(8,128)S(1)}, f32[6,24,128]{2,1,0:T(8,128)S(1)}) custom-call(s32[12,16]{1,0:T(8,128)} %neighbours_far.1, s32[12]{0:T(128)} %occupancy_far.1, s32[2,1024]{1,0:T(2,128)} %cuts_far.1, f32[12,6,128]{2,1,0:T(8,128)} %part_far.1), custom_call_target="tpu_custom_call" | custom-call | tf_op jit(solution)/shard_map/pallas_call | solution.py:350
  59.5 0.6 %copy.8 = f32[24,6,128]{2,0,1:T(8,128)} copy(f32[24,6,128]{2,0,1:T(8,128)S(1)} %bitcast.3) | data formatting | bytes 147456
  60.1 0.6 %copy.9 = f32[24,6,128]{2,0,1:T(8,128)} copy(f32[24,6,128]{2,0,1:T(8,128)S(1)} %bitcast.2) | data formatting | bytes 147456
